TPU v7x, 256 devices: a whole 4x4x8 slice. The times are simulated.
256 devices in a mesh: dp: 8 (over y, core), cent: 32 (over x, z).
Axes of the slice: x: 4, y: 4, z: 8, core: 2. Of those that a mesh axis runs over, the one named last changes fastest.
Arguments:
- passages: bfloat16 [32768, 768], P(('dp', 'cent')), may hold values from -10 to 10
- queries: bfloat16 [1024, 768], P(('dp', 'cent')), may hold values from -10 to 10
- init_centroids: float32 [8192, 768], P('cent'), may hold values from -12 to 12
- pattern: int32 [1024, 4], replicated, may hold values from 0 to 255, all different within a row
- positive_offset: int32 [1024], replicated, may hold values from 0 to 127
Outputs:
- centroids: float32 [8192, 768], P('cent')
- loss: float32 [1024], P(('dp', 'cent'))
Inputs may be any that keep to these rules, and one draw needn't show every extreme that they name: `pattern`: each row names 4 different blocks.
All inputs are finite; a program needn't handle non-finite values.
Results may differ from a plain program's by a relative error of at most 0.0055.
Values may be sent and summed in bfloat16 or wider, within the bound.
A program may use at most 64 MiB of HBM per device.

v0:
```python
import jax
import jax.numpy as jnp
from jax import lax
from jax.sharding import PartitionSpec as P

BLOCK = 128
ITERS = 2
sharpness = 0.05
sharpening_factor = 0.05
prior_weight = 1.0


def merged(value, axis, join):
    pieces = jax.tree.map(lambda part: lax.all_gather(part, axis), value)
    head = jax.tree.map(lambda part: part[0], pieces)
    tail = jax.tree.map(lambda part: part[1:], pieces)
    so_far, _ = lax.scan(lambda so_far, section: (join(so_far, section), None), head, tail)
    return so_far


def combine_query(first, second):
    upper = jnp.maximum(first[0], second[0])
    total = first[1] * jnp.exp(first[0] - upper) + second[1] * jnp.exp(second[0] - upper)
    return (upper, total, first[2] + second[2])


def on_device(passages, queries, init_centroids, pattern, positive_offset):
    gathered = lax.all_gather(passages, "cent", axis=0, tiled=True)
    cluster_means = init_centroids
    for step_index in range(ITERS):
        centers_half = cluster_means.astype(jnp.bfloat16)
        cluster_center_norms = jnp.sum(cluster_means * cluster_means, axis=1)
        unnormalized_log_odds = sharpness * (
            2.0 * jnp.dot(gathered, centers_half.T, preferred_element_type=jnp.float32)
            - cluster_center_norms[None, :]
        )
        row_max = lax.pmax(jnp.max(unnormalized_log_odds, axis=1), "cent")
        weights_exp = jnp.exp(unnormalized_log_odds - row_max[:, None])
        row_total = lax.psum(jnp.sum(weights_exp, axis=1), "cent")
        resp = weights_exp / row_total[:, None]
        numer = lax.dot_general(
            resp.astype(jnp.bfloat16),
            gathered,
            (((0,), (0,)), ((), ())),
            preferred_element_type=jnp.float32,
        )
        counts = jnp.sum(resp, axis=0)
        numer, counts = lax.psum((numer, counts), "dp")
        cluster_means = (numer + prior_weight * cluster_means) / (counts[:, None] + prior_weight)
    query_collection = lax.all_gather(queries, ("dp", "cent"), axis=0, tiled=True)
    local_rows = passages.shape[0]
    linear = lax.axis_index(("dp", "cent"))
    first_row = linear * local_rows
    local_blocks = first_row // BLOCK + jnp.arange(local_rows // BLOCK, dtype=jnp.int32)
    paired_entries = jnp.any(pattern[:, :, None] == local_blocks[None, None, :], axis=1)
    allowed = jnp.repeat(paired_entries, BLOCK, axis=1)
    affinity_matrix = (
        jnp.dot(query_collection, passages.T, preferred_element_type=jnp.float32)
        * sharpening_factor
    )
    target_col = pattern[:, 0] * BLOCK + positive_offset - first_row
    columns = jnp.arange(local_rows, dtype=jnp.int32)
    positive = jnp.sum(
        jnp.where(columns[None, :] == target_col[:, None], affinity_matrix, 0.0), axis=1
    )
    local_max = jnp.max(jnp.where(allowed, affinity_matrix, -1e30), axis=1)
    local_total = jnp.sum(
        jnp.where(allowed, jnp.exp(affinity_matrix - local_max[:, None]), 0.0), axis=1
    )
    query_max, query_total, positive_all = merged(
        (local_max, local_total, positive), ("dp", "cent"), combine_query
    )
    whole_loss = jnp.log(query_total) + query_max - positive_all
    own_count = queries.shape[0]
    own_loss = lax.dynamic_slice_in_dim(whole_loss, linear * own_count, own_count, 0)
    return (cluster_means, own_loss)


def solution(mesh):
    placed = (P(("dp", "cent"), None), P(("dp", "cent"), None), P("cent", None), P(), P())
    return jax.shard_map(
        on_device,
        mesh=mesh,
        in_specs=placed,
        out_specs=(P("cent", None), P(("dp", "cent"))),
        check_vma=False,
    )
```

profile of v0, /device:TPU:2, one launch (start us, length us, event | category | flops | bytes accessed | tf_op | source)
XLA Modules:
  0.0 1376.9 jit_solution(4740807136776224495)
XLA Ops:
  8.7 108.5 %all-gather.18.cloned.1.call-done = bf16[256,4,768]{2,1,0:T(4,128)(2,1)} async-done(((bf16[1,4,768]{2,1,0:T(4,128)(2,1)}), bf16[256,4,768]{2,1,0:T(4,128)(2,1)}) %all-gather.18.cloned.1.call-update) | async-done | bytes 1572880 | tf_op jit(solution)/shard_map/all_gather | solution.py:50
  117.2 2.7 reshape.42
  120.0 2.2 select_reduce_fusion.2
  123.0 1.4 select_reduce_fusion
  125.8 97.7 %all-gather.12.cloned.1.call-done = f32[262144]{0:T(1024)} async-done(((f32[1024]{0:T(1024)}), f32[262144]{0:T(1024)}) %all-gather.12.cloned.1.call-update) | async-done | bytes 1048592 | tf_op jit(solution)/shard_map/all_gather | solution.py:14
  223.4 1.3 slice.37
  224.9 103.3 %all-gather.14.cloned.1.call-done = f32[262144]{0:T(1024)} async-done(((f32[1024]{0:T(1024)}), f32[262144]{0:T(1024)}) %all-gather.14.cloned.1.call-update) | async-done | bytes 1048592 | tf_op jit(solution)/shard_map/all_gather | solution.py:14
  328.2 1.3 slice.38
  329.5 1.1 reshape.39
  330.6 102.2 %all-gather.16.cloned.1.call-done = f32[262144]{0:T(1024)} async-done(((f32[1024]{0:T(1024)}), f32[262144]{0:T(1024)}) %all-gather.16.cloned.1.call-update) | async-done | bytes 1048592 | tf_op jit(solution)/shard_map/all_gather | solution.py:14
  432.8 1.3 slice.39
  434.1 1.1 reshape.40
  435.2 218.6 %while.14 = (s32[]{:T(128)}, f32[1024]{0:T(1024)S(1)}, f32[1024]{0:T(1024)S(1)}, f32[1024]{0:T(1024)S(1)}, f32[255,1024]{1,0:T(8,128)S(1)}, /*index=5*/f32[255,1024]{1,0:T(8,128)}, f32[255,1024]{1,0:T(8,128)}, s32[]{:T(128)}) while((s32[]{:T(128)}, f32[1024]{0:T(1024)S(1)}, f32[1024]{0:T(1024)S(1)}, f32[1024]{0:T(1024)S(1)}, ...), condition=%wide.region_21.22_spmd, body=%wide.region_20.21_spmd.sunk | while | flops 7170 | bytes 61541 | solution.py:17
  435.3 0.8 constant_dynamic-slice_fusion.5
  436.1 0.8 constant_dynamic-slice_fusion.5
  445.5 0.8 constant_dynamic-slice_fusion.5
  446.4 0.8 constant_dynamic-slice_fusion.5
  447.3 0.8 constant_dynamic-slice_fusion.5
  452.4 0.8 constant_dynamic-slice_fusion.5
  455.8 0.8 constant_dynamic-slice_fusion.5
  460.1 0.8 constant_dynamic-slice_fusion.5
  463.6 0.8 constant_dynamic-slice_fusion.5
  466.1 0.8 constant_dynamic-slice_fusion.5
  467.0 0.8 constant_dynamic-slice_fusion.5
  484.1 0.8 constant_dynamic-slice_fusion.5
  485.0 0.8 constant_dynamic-slice_fusion.5
  490.1 0.8 constant_dynamic-slice_fusion.5
  491.0 0.8 constant_dynamic-slice_fusion.5
  491.9 0.8 constant_dynamic-slice_fusion.5
  493.6 0.8 constant_dynamic-slice_fusion.5
  495.3 0.8 constant_dynamic-slice_fusion.5
  496.2 0.8 constant_dynamic-slice_fusion.5
  497.0 0.8 constant_dynamic-slice_fusion.5
  499.6 0.8 constant_dynamic-slice_fusion.5
  502.2 0.8 constant_dynamic-slice_fusion.5
  503.0 0.8 constant_dynamic-slice_fusion.5
  503.9 0.8 constant_dynamic-slice_fusion.5
  504.7 0.8 constant_dynamic-slice_fusion.5
  505.6 0.8 constant_dynamic-slice_fusion.5
  507.3 0.8 constant_dynamic-slice_fusion.5
  511.6 0.8 constant_dynamic-slice_fusion.5
  512.5 0.8 constant_dynamic-slice_fusion.5
  513.3 0.8 constant_dynamic-slice_fusion.5
  515.9 0.8 constant_dynamic-slice_fusion.5
  516.8 0.8 constant_dynamic-slice_fusion.5
  517.6 0.8 constant_dynamic-slice_fusion.5
  654.5 6.7 fusion.18
  661.1 130.3 %pmax.14 = f32[4096]{0:T(1024)S(1)} all-reduce(f32[4096]{0:T(1024)S(1)} %get-tuple-element.66), channel_id=1, replica_groups=mesh['dp'=8,'cent'=32] {'cent'}, use_global_device_ids=true, to_apply=%region_2.0 | all-reduce | flops 4096 | bytes 32768 | tf_op jit(solution)/shard_map/pmax | solution.py:37
  791.4 2.8 fusion.5
  794.2 137.7 %psum.42 = f32[4096]{0:T(1024)S(1)} all-reduce(f32[4096]{0:T(1024)S(1)} %fusion.5), channel_id=1, replica_groups=mesh['dp'=8,'cent'=32] {'cent'}, use_global_device_ids=true, to_apply=%region_4.0 | all-reduce | flops 4096 | bytes 32768 | tf_op jit(solution)/shard_map/psum | solution.py:39
  931.8 6.8 fusion.10
  938.7 3.0 fusion.14
  941.7 12.4 psum.44
  954.1 57.1 %all-reduce.3.cloned.1.call-done = f32[256,768]{1,0:T(8,128)} async-done(((f32[256,768]{1,0:T(8,128)}), f32[256,768]{1,0:T(8,128)}) %all-reduce.3.cloned.1.call-update) | async-done | bytes 786448 | tf_op jit(solution)/shard_map/psum | solution.py:48
  1011.3 1.4 multiply_reduce_fusion
  1012.6 6.7 fusion.19
  1019.3 131.0 %pmax.15 = f32[4096]{0:T(1024)S(1)} all-reduce(f32[4096]{0:T(1024)S(1)} %get-tuple-element.68), channel_id=1, replica_groups=mesh['dp'=8,'cent'=32] {'cent'}, use_global_device_ids=true, to_apply=%region_10.0 | all-reduce | flops 4096 | bytes 32768 | tf_op jit(solution)/shard_map/pmax | solution.py:37
  1150.3 2.8 fusion.6
  1153.1 137.9 %psum.45 = f32[4096]{0:T(1024)S(1)} all-reduce(f32[4096]{0:T(1024)S(1)} %fusion.6), channel_id=1, replica_groups=mesh['dp'=8,'cent'=32] {'cent'}, use_global_device_ids=true, to_apply=%region_12.0 | all-reduce | flops 4096 | bytes 32768 | tf_op jit(solution)/shard_map/psum | solution.py:39
  1291.0 6.8 fusion.8
  1297.8 3.0 fusion.12
  1300.8 12.4 psum.47
  1313.2 54.7 %all-reduce.5.cloned.1.call-done = f32[256,768]{1,0:T(8,128)} async-done(((f32[256,768]{1,0:T(8,128)}), f32[256,768]{1,0:T(8,128)}) %all-reduce.5.cloned.1.call-update) | async-done | bytes 786448 | tf_op jit(solution)/shard_map/psum | solution.py:48
  1367.9 2.1 add_divide_fusion
  (1021 shorter events, 187.0 us)
Async XLA Ops:
  7.2 115.8 %copy-start.1 = (s32[1024]{0:T(1024)S(1)}, s32[1024]{0:T(1024)}, u32[]{:S(2)}) copy-start(s32[1024]{0:T(1024)} %param.11) | copy-start | bytes 12292
  7.2 118.5 %copy-start = (f32[256,768]{1,0:T(8,128)S(1)}, f32[256,768]{1,0:T(8,128)}, u32[]{:S(2)}) copy-start(f32[256,768]{1,0:T(8,128)} %param.9) | copy-start | bytes 2359300
  7.2 110.0 %all-gather.18.cloned.1.call-start = ((), (), s32[]{:S(2)}) async-start(), calls=%async_computation.6 | async-start | bytes 1579008 | tf_op jit(solution)/shard_map/all_gather | solution.py:50
  7.9 215.5 %all-gather.12.cloned.1.call-start = ((), (), s32[]{:S(2)}) async-start(), calls=%async_computation.3 | async-start | bytes 1052672 | tf_op jit(solution)/shard_map/all_gather | solution.py:14
  122.2 206.0 %all-gather.14.cloned.1.call-start = ((), (), s32[]{:S(2)}) async-start(), calls=%async_computation.4 | async-start | bytes 1052672 | tf_op jit(solution)/shard_map/all_gather | solution.py:14
  124.4 308.4 %all-gather.16.cloned.1.call-start = ((), (), s32[]{:S(2)}) async-start(), calls=%async_computation.5 | async-start | bytes 1052672 | tf_op jit(solution)/shard_map/all_gather | solution.py:14
  125.0 529.4 %all-gather.10.cloned.1.call-start = ((), (), s32[]{:S(2)}) async-start(), calls=%async_computation | async-start | bytes 6488064 | tf_op jit(solution)/shard_map/all_gather | solution.py:28
  125.6 885.7 %all-reduce.3.cloned.1.call-start = ((), (), s32[]{:S(2)}) async-start(), calls=%async_computation.1 | async-start | bytes 1572864 | tf_op jit(solution)/shard_map/psum | solution.py:48
  224.9 210.3 %slice-start = ((f32[262144]{0:T(1024)}), f32[1024]{0:T(1024)S(1)}, s32[]{:S(2)}) async-start(f32[262144]{0:T(1024)} %all-gather.12.cloned.1.call-done), calls=%async_computation.7 | async-start | bytes 8192 | tf_op jit(solution)/shard_map/slice | solution.py:15
  328.2 107.0 %slice-start.1 = ((f32[262144]{0:T(1024)}), f32[1024]{0:T(1024)S(1)}, s32[]{:S(2)}) async-start(f32[262144]{0:T(1024)} %all-gather.14.cloned.1.call-done), calls=%async_computation.8 | async-start | bytes 8192 | tf_op jit(solution)/shard_map/slice | solution.py:15
  432.8 2.4 slice-start.2
  938.7 429.2 %all-reduce.5.cloned.1.call-start = ((), (), s32[]{:S(2)}) async-start(), calls=%async_computation.2 | async-start | bytes 1572864 | tf_op jit(solution)/shard_map/psum | solution.py:48
Sparse Core Ops, SparseCore 0:
  11.6 105.6 all-gather.17
  122.3 101.0 all-gather.11
  227.2 100.9 all-gather.13
  331.8 100.9 all-gather.15
  435.2 86.4 all-gather.9
  938.8 72.4 all-reduce.2
  1297.9 69.9 all-reduce.4
where the time goes:
time: 1400 us; the launch traced here: 1380 us
  blocking collectives  562 us (40%)
  waiting for transfers between devices  525 us (38%)
  local copies, waits for them, and re-layouts  214 us (15%)
  matrix products  29.1 us (2%)
  other arithmetic  22.3 us (2%)
  between operations  14.2 us (1%)
    all_gather x3, waiting for transfers between devices, merged(): pieces = jax.tree.map(lambda part: lax.all_gather(part, axis), value)  303 us
    psum x2, blocking collectives, on_device(): row_total = lax.psum(jnp.sum(weights_exp, axis=1), 'cent')  276 us
    pmax x2, blocking collectives, on_device(): row_max = lax.pmax(jnp.max(unnormalized_log_odds, axis=1), 'cent')  261 us
    dynamic_slice x510, local copies, waits for them, and re-layouts, merged(): lax.scan(lambda so_far, section: (join(so_far, section), None), head, tail)  205 us
    psum x2, waiting for transfers between devices, on_device(): numer, counts = lax.psum((numer, counts), 'dp')  112 us
    all_gather x1, waiting for transfers between devices, on_device(): lax.all_gather(queries, ('dp', 'cent'), axis=0, tiled=True)  109 us
  transfers between devices with their start and end apart: 7, of which 6 were waited for; matrix products, arithmetic and copies ran while one was open for 16% of the time, Pallas kernels for 0%

commit v1 on v0

--- a/solution.py
+++ b/solution.py
@@ -47,7 +47,15 @@
         counts = jnp.sum(resp, axis=0)
         numer, counts = lax.psum((numer, counts), "dp")
         cluster_means = (numer + prior_weight * cluster_means) / (counts[:, None] + prior_weight)
-    query_collection = lax.all_gather(queries, ("dp", "cent"), axis=0, tiled=True)
+    query_collection = jnp.concatenate(
+        jax.lax.all_to_all(
+            jnp.stack([queries] * jax.lax.axis_size(("dp", "cent"))),
+            ("dp", "cent"),
+            split_axis=0,
+            concat_axis=0,
+        ),
+        axis=0,
+    )
     local_rows = passages.shape[0]
     linear = lax.axis_index(("dp", "cent"))
     first_row = linear * local_rows

time: 1400 us -> 1340 us (0.957)
  waiting for transfers between devices: 525 us -> 455 us
  starting transfers between devices: 0.28 us -> 14.9 us
    all_gather x1 -> x0, waiting for transfers between devices: 109 us -> none  [on_device(): lax.all_gather(queries, ('dp', 'cent'), axis=0, tiled=True)]
    all_to_all x0 -> x1, waiting for transfers between devices: none -> 42.4 us  [on_device(): jax.lax.all_to_all(jnp.stack([queries] * jax.lax.axis_size(('dp', 'cent')...]
    all_to_all x0 -> x1, starting transfers between devices: none -> 14.7 us  [on_device(): jax.lax.all_to_all(jnp.stack([queries] * jax.lax.axis_size(('dp', 'cent')...]
  transfers between devices with their start and end apart: 7 -> 7, of which waited for: 6 -> 6; matrix products, arithmetic and copies ran while one was open for 16% -> 17% of each run, Pallas kernels for 0% -> 0%
where the time goes in v1:
time: 1340 us; the launch traced here: 1320 us
  blocking collectives  562 us (42%)
  waiting for transfers between devices  455 us (34%)
  local copies, waits for them, and re-layouts  215 us (16%)
  matrix products  29.6 us (2%)
  other arithmetic  20.8 us (2%)
  starting transfers between devices  14.9 us (1%)
  between operations  14.2 us (1%)
    all_gather x3, waiting for transfers between devices, merged(): pieces = jax.tree.map(lambda part: lax.all_gather(part, axis), value)  299 us
    psum x2, blocking collectives, on_device(): row_total = lax.psum(jnp.sum(weights_exp, axis=1), 'cent')  276 us
    pmax x2, blocking collectives, on_device(): row_max = lax.pmax(jnp.max(unnormalized_log_odds, axis=1), 'cent')  261 us
    dynamic_slice x510, local copies, waits for them, and re-layouts, merged(): lax.scan(lambda so_far, section: (join(so_far, section), None), head, tail)  205 us
    psum x2, waiting for transfers between devices, on_device(): numer, counts = lax.psum((numer, counts), 'dp')  112 us
    all_to_all x1, waiting for transfers between devices, on_device(): jax.lax.all_to_all(jnp.stack([queries] * jax.lax.axis_size(('dp', 'cent')...  42.4 us
  transfers between devices with their start and end apart: 7, of which 6 were waited for; matrix products, arithmetic and copies ran while one was open for 17% of the time, Pallas kernels for 0%

profile of v1, /device:TPU:2, one launch (start us, length us, event | category | flops | bytes accessed | tf_op | source)
XLA Modules:
  0.0 1320.8 jit_solution(7963242228436642097)
XLA Ops:
  7.2 2.3 stack.2
  9.5 14.7 %all-to-all-start = ((bf16[256,4,768]{2,1,0:T(4,128)(2,1)}), bf16[256,4,768]{2,1,0:T(4,128)(2,1)S(1)}, u32[]{:S(2)}, u32[]{:S(2)}) async-start(bf16[256,4,768]{2,1,0:T(4,128)(2,1)} %stack.2), calls=%async_computation | async-start | bytes 3145728 | tf_op jit(solution)/shard_map/all_to_all | solution.py:51
  24.3 42.4 %all-to-all-done = bf16[256,4,768]{2,1,0:T(4,128)(2,1)S(1)} async-done(((bf16[256,4,768]{2,1,0:T(4,128)(2,1)}), bf16[256,4,768]{2,1,0:T(4,128)(2,1)S(1)}, u32[]{:S(2)}, u32[]{:S(2)}) %all-to-all-start) | async-done | bytes 1572896 | tf_op jit(solution)/shard_map/all_to_all | solution.py:51
  66.7 1.3 reshape.34
  68.1 2.7 select_reduce_fusion.2
  70.8 1.4 select_reduce_fusion
  73.8 93.5 %all-gather.10.cloned.1.call-done = f32[262144]{0:T(1024)} async-done(((f32[1024]{0:T(1024)}), f32[262144]{0:T(1024)}) %all-gather.10.cloned.1.call-update) | async-done | bytes 1048592 | tf_op jit(solution)/shard_map/all_gather | solution.py:14
  167.3 1.3 slice.37
  168.7 103.3 %all-gather.12.cloned.1.call-done = f32[262144]{0:T(1024)} async-done(((f32[1024]{0:T(1024)}), f32[262144]{0:T(1024)}) %all-gather.12.cloned.1.call-update) | async-done | bytes 1048592 | tf_op jit(solution)/shard_map/all_gather | solution.py:14
  272.0 1.3 slice.38
  273.3 1.1 reshape.45
  274.4 102.3 %all-gather.14.cloned.1.call-done = f32[262144]{0:T(1024)} async-done(((f32[1024]{0:T(1024)}), f32[262144]{0:T(1024)}) %all-gather.14.cloned.1.call-update) | async-done | bytes 1048592 | tf_op jit(solution)/shard_map/all_gather | solution.py:14
  376.8 1.3 slice.39
  378.1 1.1 reshape.46
  379.2 218.6 %while.14 = (s32[]{:T(128)}, f32[1024]{0:T(1024)S(1)}, f32[1024]{0:T(1024)S(1)}, f32[1024]{0:T(1024)S(1)}, f32[255,1024]{1,0:T(8,128)S(1)}, /*index=5*/f32[255,1024]{1,0:T(8,128)}, f32[255,1024]{1,0:T(8,128)}, s32[]{:T(128)}) while((s32[]{:T(128)}, f32[1024]{0:T(1024)S(1)}, f32[1024]{0:T(1024)S(1)}, f32[1024]{0:T(1024)S(1)}, ...), condition=%wide.region_21.22_spmd, body=%wide.region_20.21_spmd.sunk | while | flops 7170 | bytes 61541 | solution.py:17
  380.1 0.8 constant_dynamic-slice_fusion.5
  389.5 0.8 constant_dynamic-slice_fusion.5
  390.4 0.8 constant_dynamic-slice_fusion.5
  391.2 0.8 constant_dynamic-slice_fusion.5
  396.4 0.8 constant_dynamic-slice_fusion.5
  399.8 0.8 constant_dynamic-slice_fusion.5
  404.1 0.8 constant_dynamic-slice_fusion.5
  407.5 0.8 constant_dynamic-slice_fusion.5
  410.1 0.8 constant_dynamic-slice_fusion.5
  410.9 0.8 constant_dynamic-slice_fusion.5
  428.1 0.8 constant_dynamic-slice_fusion.5
  429.0 0.8 constant_dynamic-slice_fusion.5
  434.1 0.8 constant_dynamic-slice_fusion.5
  435.0 0.8 constant_dynamic-slice_fusion.5
  435.8 0.8 constant_dynamic-slice_fusion.5
  437.5 0.8 constant_dynamic-slice_fusion.5
  439.3 0.8 constant_dynamic-slice_fusion.5
  440.1 0.8 constant_dynamic-slice_fusion.5
  441.0 0.8 constant_dynamic-slice_fusion.5
  443.6 0.8 constant_dynamic-slice_fusion.5
  446.1 0.8 constant_dynamic-slice_fusion.5
  447.0 0.8 constant_dynamic-slice_fusion.5
  447.8 0.8 constant_dynamic-slice_fusion.5
  448.7 0.8 constant_dynamic-slice_fusion.5
  449.6 0.8 constant_dynamic-slice_fusion.5
  451.3 0.8 constant_dynamic-slice_fusion.5
  455.6 0.8 constant_dynamic-slice_fusion.5
  456.4 0.8 constant_dynamic-slice_fusion.5
  459.9 0.8 constant_dynamic-slice_fusion.5
  460.7 0.8 constant_dynamic-slice_fusion.5
  461.6 0.8 constant_dynamic-slice_fusion.5
  598.4 6.7 fusion.18
  605.1 130.2 %pmax.14 = f32[4096]{0:T(1024)S(1)} all-reduce(f32[4096]{0:T(1024)S(1)} %get-tuple-element.66), channel_id=1, replica_groups=mesh['dp'=8,'cent'=32] {'cent'}, use_global_device_ids=true, to_apply=%region_2.0 | all-reduce | flops 4096 | bytes 32768 | tf_op jit(solution)/shard_map/pmax | solution.py:37
  735.3 2.8 fusion.5
  738.1 137.7 %psum.42 = f32[4096]{0:T(1024)S(1)} all-reduce(f32[4096]{0:T(1024)S(1)} %fusion.5), channel_id=1, replica_groups=mesh['dp'=8,'cent'=32] {'cent'}, use_global_device_ids=true, to_apply=%region_4.0 | all-reduce | flops 4096 | bytes 32768 | tf_op jit(solution)/shard_map/psum | solution.py:39
  875.8 6.8 fusion.10
  882.7 3.0 fusion.14
  885.6 12.4 psum.44
  898.1 57.2 %all-reduce.3.cloned.1.call-done = f32[256,768]{1,0:T(8,128)} async-done(((f32[256,768]{1,0:T(8,128)}), f32[256,768]{1,0:T(8,128)}) %all-reduce.3.cloned.1.call-update) | async-done | bytes 786448 | tf_op jit(solution)/shard_map/psum | solution.py:48
  955.2 1.4 multiply_reduce_fusion
  956.6 6.7 fusion.19
  963.3 131.0 %pmax.15 = f32[4096]{0:T(1024)S(1)} all-reduce(f32[4096]{0:T(1024)S(1)} %get-tuple-element.68), channel_id=1, replica_groups=mesh['dp'=8,'cent'=32] {'cent'}, use_global_device_ids=true, to_apply=%region_10.0 | all-reduce | flops 4096 | bytes 32768 | tf_op jit(solution)/shard_map/pmax | solution.py:37
  1094.3 2.8 fusion.6
  1097.1 137.9 %psum.45 = f32[4096]{0:T(1024)S(1)} all-reduce(f32[4096]{0:T(1024)S(1)} %fusion.6), channel_id=1, replica_groups=mesh['dp'=8,'cent'=32] {'cent'}, use_global_device_ids=true, to_apply=%region_12.0 | all-reduce | flops 4096 | bytes 32768 | tf_op jit(solution)/shard_map/psum | solution.py:39
  1234.9 6.8 fusion.8
  1241.8 3.0 fusion.12
  1244.7 12.4 psum.47
  1257.2 54.7 %all-reduce.5.cloned.1.call-done = f32[256,768]{1,0:T(8,128)} async-done(((f32[256,768]{1,0:T(8,128)}), f32[256,768]{1,0:T(8,128)}) %all-reduce.5.cloned.1.call-update) | async-done | bytes 786448 | tf_op jit(solution)/shard_map/psum | solution.py:48
  1311.8 2.1 add_divide_fusion
  (1025 shorter events, 186.6 us)
Async XLA Ops:
  7.2 17.1 %copy-start.2 = (s32[1024,4]{0,1:T(4,128)S(1)}, s32[1024,4]{0,1:T(4,128)}, u32[]{:S(2)}) copy-start(s32[1024,4]{0,1:T(4,128)} %param.10) | copy-start | bytes 49156
  7.2 60.9 %copy-start.1 = (bf16[128,768]{1,0:T(8,128)(2,1)S(1)}, bf16[128,768]{1,0:T(8,128)(2,1)}, u32[]{:S(2)}) copy-start(bf16[128,768]{1,0:T(8,128)(2,1)} %param.7) | copy-start | bytes 589828
  9.5 61.3 %copy-start.3 = (s32[1024]{0:T(1024)S(1)}, s32[1024]{0:T(1024)}, u32[]{:S(2)}) copy-start(s32[1024]{0:T(1024)} %param.11) | copy-start | bytes 12292
  9.5 64.2 %copy-start = (f32[256,768]{1,0:T(8,128)S(1)}, f32[256,768]{1,0:T(8,128)}, u32[]{:S(2)}) copy-start(f32[256,768]{1,0:T(8,128)} %param.9) | copy-start | bytes 2359300
  9.5 57.2 %all-to-all-start = ((bf16[256,4,768]{2,1,0:T(4,128)(2,1)}), bf16[256,4,768]{2,1,0:T(4,128)(2,1)S(1)}, u32[]{:S(2)}, u32[]{:S(2)}) async-start(bf16[256,4,768]{2,1,0:T(4,128)(2,1)} %stack.2), calls=%async_computation | async-start | bytes 3145728 | tf_op jit(solution)/shard_map/all_to_all | solution.py:51
  24.2 143.1 %all-gather.10.cloned.1.call-start = ((), (), s32[]{:S(2)}) async-start(), calls=%async_computation.4 | async-start | bytes 1052672 | tf_op jit(solution)/shard_map/all_gather | solution.py:14
  70.7 201.3 %all-gather.12.cloned.1.call-start = ((), (), s32[]{:S(2)}) async-start(), calls=%async_computation.5 | async-start | bytes 1052672 | tf_op jit(solution)/shard_map/all_gather | solution.py:14
  72.3 304.5 %all-gather.14.cloned.1.call-start = ((), (), s32[]{:S(2)}) async-start(), calls=%async_computation.6 | async-start | bytes 1052672 | tf_op jit(solution)/shard_map/all_gather | solution.py:14
  73.0 525.4 %all-gather.8.cloned.1.call-start = ((), (), s32[]{:S(2)}) async-start(), calls=%async_computation.1 | async-start | bytes 6488064 | tf_op jit(solution)/shard_map/all_gather | solution.py:28
  73.6 881.6 %all-reduce.3.cloned.1.call-start = ((), (), s32[]{:S(2)}) async-start(), calls=%async_computation.2 | async-start | bytes 1572864 | tf_op jit(solution)/shard_map/psum | solution.py:48
  168.7 210.5 %slice-start = ((f32[262144]{0:T(1024)}), f32[1024]{0:T(1024)S(1)}, s32[]{:S(2)}) async-start(f32[262144]{0:T(1024)} %all-gather.10.cloned.1.call-done), calls=%async_computation.7 | async-start | bytes 8192 | tf_op jit(solution)/shard_map/slice | solution.py:15
  272.0 107.2 %slice-start.1 = ((f32[262144]{0:T(1024)}), f32[1024]{0:T(1024)S(1)}, s32[]{:S(2)}) async-start(f32[262144]{0:T(1024)} %all-gather.12.cloned.1.call-done), calls=%async_computation.8 | async-start | bytes 8192 | tf_op jit(solution)/shard_map/slice | solution.py:15
  376.8 2.4 slice-start.2
  882.6 429.2 %all-reduce.5.cloned.1.call-start = ((), (), s32[]{:S(2)}) async-start(), calls=%async_computation.3 | async-start | bytes 1572864 | tf_op jit(solution)/shard_map/psum | solution.py:48
Sparse Core Ops, SparseCore 0:
  70.9 96.3 all-gather.9
  171.0 100.9 all-gather.11
  275.8 100.9 all-gather.13
  379.2 86.4 all-gather.7
  882.7 72.4 all-reduce.2
  1241.9 69.8 all-reduce.4
